TPU v7x, 32 devices: a whole 2x2x4 slice. The times are simulated.
32 devices in a mesh: freq: 8 (over z, y), tm: 4 (over x, core).
Axes of the slice: x: 2, y: 2, z: 4, core: 2. Of those that a mesh axis runs over, the one named last changes fastest.
Arguments:
- visibility: bfloat16 [8, 4, 8, 4096], P('freq', 'tm'), may hold values from -6 to 6
- model_visibility: bfloat16 [8, 4, 8, 4096], P('freq', 'tm'), may hold values from -6 to 6
- keep_mask: int32 [8, 4, 4096], P('freq', 'tm'), may hold values 0 or 1
- gains_in: float32 [8, 8, 512], P('freq'), may hold values from -6 to 6
- consensus_in: float32 [8, 8, 512], P('freq'), may hold values from -6 to 6
- dual_in: float32 [8, 8, 512], P('freq'), may hold values from -4 to 4
- penalty: float32 [512], replicated, may hold values from 30 to 600
- channel_index: int32 [8], P('freq'), may hold values from 0 to 7, each once
- first_station: int32 [4096], replicated, may hold values from 0 to 511, as said below
- second_station: int32 [4096], replicated, may hold values from 0 to 511
Outputs:
- gains_out: float32 [8, 8, 512], P('freq', None, 'tm')
- consensus_out: float32 [8, 8, 512], P('freq', None, 'tm')
- dual_out: float32 [8, 8, 512], P('freq', None, 'tm')
Inputs may be any that keep to these rules, and one draw needn't show every extreme that they name: first_station and second_station of a baseline differ; station numbers repeat over baselines. channel_index holds each channel number once.
All inputs are finite; a program needn't handle non-finite values. No bound on the sum of `keep_mask` on one device may be relied on, other than what follows from the above.
Results may differ from a plain program's by a relative error of at most 0.0003.
Values sent between devices are 32-bit elements; how exact they have to be, the bound alone decides.
No kernel may reach another device: no remote copies, remote signals or barrier semaphores. Data moves between devices by JAX's collectives and lax.ppermute only.
A program may use at most 64 MiB of HBM per device.

v0:
```python
import jax
import jax.numpy as jnp
from jax import lax
from jax.sharding import PartitionSpec as P

SWEEPS = 2


def entries(array, axis):
    return [
        (
            lax.index_in_dim(array, 2 * index, axis, False),
            lax.index_in_dim(array, 2 * index + 1, axis, False),
        )
        for index in range(4)
    ]


def stack_jones(matrix, axis):
    return jnp.stack([matrix[index][part] for index in range(4) for part in range(2)], axis=axis)


def complex_mul(leading_entry, second):
    return (
        leading_entry[0] * second[0] - leading_entry[1] * second[1],
        leading_entry[0] * second[1] + leading_entry[1] * second[0],
    )


def complex_add(leading_entry, second):
    return (leading_entry[0] + second[0], leading_entry[1] + second[1])


def matrix_mul(leading_entry, second):
    return [
        complex_add(
            complex_mul(leading_entry[0], second[0]), complex_mul(leading_entry[1], second[2])
        ),
        complex_add(
            complex_mul(leading_entry[0], second[1]), complex_mul(leading_entry[1], second[3])
        ),
        complex_add(
            complex_mul(leading_entry[2], second[0]), complex_mul(leading_entry[3], second[2])
        ),
        complex_add(
            complex_mul(leading_entry[2], second[1]), complex_mul(leading_entry[3], second[3])
        ),
    ]


def adjoint(matrix):
    return [
        (matrix[0][0], -matrix[0][1]),
        (matrix[2][0], -matrix[2][1]),
        (matrix[1][0], -matrix[1][1]),
        (matrix[3][0], -matrix[3][1]),
    ]


def weighted(matrix, weight):
    return [(entry[0] * weight, entry[1] * weight) for entry in matrix]


def one_hot_table(station_list, stations):
    return (jnp.arange(stations, dtype=jnp.int32)[:, None] == station_list[None, :]).astype(
        jnp.float32
    )


def normal_sums(vis_block, model_block, flag_block, gains, first_hot, second_hot):
    gains_first = jnp.einsum("cjs,sb->cjb", gains, first_hot, precision=lax.Precision.HIGHEST)[
        :, None
    ]
    gains_second = jnp.einsum("cjs,sb->cjb", gains, second_hot, precision=lax.Precision.HIGHEST)[
        :, None
    ]
    observed = entries(vis_block.astype(jnp.float32), 2)
    modelled = entries(model_block.astype(jnp.float32), 2)
    weight = flag_block.astype(jnp.float32)
    left = matrix_mul(modelled, adjoint(entries(gains_second, 2)))
    right = matrix_mul(adjoint(modelled), adjoint(entries(gains_first, 2)))
    num_first = weighted(matrix_mul(observed, adjoint(left)), weight)
    den_first = weighted(matrix_mul(left, adjoint(left)), weight)
    num_second = weighted(matrix_mul(adjoint(observed), adjoint(right)), weight)
    den_second = weighted(matrix_mul(right, adjoint(right)), weight)
    term_first = jnp.sum(
        jnp.concatenate([stack_jones(num_first, 1), stack_jones(den_first, 1)], axis=1), axis=2
    )
    term_second = jnp.sum(
        jnp.concatenate([stack_jones(num_second, 1), stack_jones(den_second, 1)], axis=1), axis=2
    )
    totals = jnp.einsum("cjb,sb->cjs", term_first, first_hot, precision=lax.Precision.HIGHEST)
    return totals + jnp.einsum(
        "cjb,sb->cjs", term_second, second_hot, precision=lax.Precision.HIGHEST
    )


def solve_jones(totals, gains_old, consensus, dual, penalty):
    numer = entries(totals[:, :8], 1)
    denom = entries(totals[:, 8:], 1)
    target = entries(consensus - dual, 1)
    rhs_side = [
        (numer[index][0] + penalty * target[index][0], numer[index][1] + penalty * target[index][1])
        for index in range(4)
    ]
    regular = [
        (denom[0][0] + penalty, denom[0][1]),
        denom[1],
        denom[2],
        (denom[3][0] + penalty, denom[3][1]),
    ]
    determ = complex_add(
        complex_mul(regular[0], regular[3]),
        complex_mul((-regular[1][0], -regular[1][1]), regular[2]),
    )
    magnitude = determ[0] * determ[0] + determ[1] * determ[1]
    recip = (determ[0] / magnitude, -determ[1] / magnitude)
    inverse = [
        complex_mul(regular[3], recip),
        complex_mul((-regular[1][0], -regular[1][1]), recip),
        complex_mul((-regular[2][0], -regular[2][1]), recip),
        complex_mul(regular[0], recip),
    ]
    solved = stack_jones(matrix_mul(rhs_side, inverse), 1)
    return 0.5 * (solved + gains_old)


def legendre(position):
    square = position * position
    return jnp.stack(
        [jnp.ones_like(position), position, 1.5 * square - 0.5, (2.5 * square - 1.5) * position],
        axis=-1,
    )


def channel_basis(index, total):
    return legendre(2.0 * index.astype(jnp.float32) / (total - 1.0) - 1.0)


def poly_fit(moments, total):
    basis_all = channel_basis(jnp.arange(total, dtype=jnp.int32), float(total))
    gram = jnp.dot(basis_all.T, basis_all, precision=lax.Precision.HIGHEST)
    factor = jnp.linalg.cholesky(gram)
    flat = moments.reshape(4, -1)
    middle = lax.linalg.triangular_solve(factor, flat, left_side=True, lower=True)
    coeffs = lax.linalg.triangular_solve(
        factor, middle, left_side=True, lower=True, transpose_a=True
    )
    return coeffs.reshape(moments.shape)


def shards(
    visibility,
    model_visibility,
    keep_mask,
    gains_in,
    consensus_in,
    dual_in,
    penalty,
    channel_index,
    first_station,
    second_station,
):
    stations = gains_in.shape[2]
    width = stations // lax.axis_size("tm")
    start_shift = lax.axis_index("tm") * width
    first_hot = one_hot_table(first_station, stations)
    second_hot = one_hot_table(second_station, stations)

    def own_part(array):
        return lax.dynamic_slice_in_dim(array, start_shift, width, array.ndim - 1)

    current = gains_in
    for sweep_index in range(SWEEPS):
        totals = normal_sums(
            visibility, model_visibility, keep_mask, current, first_hot, second_hot
        )
        summed = lax.psum(totals, "tm")
        current = solve_jones(summed, current, consensus_in, dual_in, penalty)
    gains_part = own_part(current)
    dual_part = own_part(dual_in)
    total_channels = channel_index.shape[0] * lax.axis_size("freq")
    basis = channel_basis(channel_index, float(total_channels))
    combined = gains_part + dual_part
    local_moments = jnp.einsum("fk,fjs->kjs", basis, combined, precision=lax.Precision.HIGHEST)
    moments = lax.psum(local_moments, "freq")
    coeffs = poly_fit(moments, total_channels)
    consensus_out = jnp.einsum("fk,kjs->fjs", basis, coeffs, precision=lax.Precision.HIGHEST)
    dual_out = dual_part + gains_part - consensus_out
    return (gains_part, consensus_out, dual_out)


def solution(mesh):
    placed = (
        P("freq", "tm", None, None),
        P("freq", "tm", None, None),
        P("freq", "tm", None),
        P("freq", None, None),
        P("freq", None, None),
        P("freq", None, None),
        P(),
        P("freq"),
        P(),
        P(),
    )
    return jax.shard_map(
        shards,
        mesh=mesh,
        in_specs=placed,
        out_specs=(P("freq", None, "tm"), P("freq", None, "tm"), P("freq", None, "tm")),
        check_vma=False,
    )
```

profile of v0, /device:TPU:0, one launch (start us, length us, event | category | flops | bytes accessed | tf_op | source)
XLA Modules:
  0.0 103.6 jit_solution(14120705225545996013)
XLA Ops:
  0.6 0.9 convert_element_type.39
  1.5 0.9 convert_element_type.40
  2.4 3.4 %fusion.10 = f32[1,1,8,4096]{3,2,1,0:T(8,128)S(1)} fusion(s32[4096]{0:T(1024)} %param.18, f32[1,8,512]{2,1,0:T(8,128)} %param.13), kind=kOutput, calls=%fused_computation.12 | convolution fusion | flops 203423744 | bytes 163840 | tf_op jit(solution)/shard_map/cjs,sb->cjb/dot_general | solution.py:71
  5.7 0.3 constant_dynamic-update-slice_fusion.31
  6.1 0.1 constant_dynamic-update-slice_fusion.30
  6.2 0.3 constant_dynamic-update-slice_fusion.29
  6.5 0.1 constant_dynamic-update-slice_fusion.28
  6.6 0.1 constant_dynamic-update-slice_fusion.27
  6.7 0.1 constant_dynamic-update-slice_fusion.26
  6.8 0.1 constant_dynamic-update-slice_fusion.25
  6.9 2.7 %fusion.8 = f32[1,1,8,4096]{3,2,1,0:T(8,128)S(1)} fusion(s32[4096]{0:T(1024)S(1)} %copy-done.8, f32[1,8,512]{2,1,0:T(8,128)S(1)} %copy-done.4), kind=kOutput, calls=%fused_computation.10 | convolution fusion | flops 203423744 | bytes 163840 | tf_op jit(solution)/shard_map/cjs,sb->cjb/dot_general | solution.py:74
  9.6 0.3 constant_dynamic-update-slice_fusion.15
  9.9 0.2 constant_dynamic-update-slice_fusion.24
  10.2 0.1 constant_dynamic-update-slice_fusion.21
  10.3 0.1 constant_dynamic-update-slice_fusion.19
  10.4 0.1 constant_dynamic-update-slice_fusion.18
  10.5 0.3 constant_dynamic-update-slice_fusion.13
  10.9 0.1 constant_dynamic-update-slice_fusion.16
  11.0 0.1 constant_dynamic-update-slice_fusion.11
  11.1 0.1 constant_dynamic-update-slice_fusion.10
  11.2 0.1 constant_dynamic-update-slice_fusion.9
  11.3 0.1 constant_dynamic-update-slice_fusion.8
  11.5 0.1 constant_dynamic-update-slice_fusion.5
  11.7 0.1 constant_dynamic-update-slice_fusion.3
  11.9 0.1 copy-done.7
  12.1 3.8 %fusion.3 = f32[16,512]{1,0:T(8,128)S(1)} fusion(s32[4096]{0:T(1024)S(1)} %copy-done.7, f32[1,16,1,4096]{3,2,1,0:T(1,128)S(1)} %constant_dynamic-update-slice_fusion), kind=kOutput, calls=%fused_computation.4 | convolution fusion | flops 404750336 | bytes 311296 | tf_op jit(solution)/shard_map/cjb,sb->cjs/dot_general | solution.py:92
  16.0 4.0 %fusion.21 = f32[1,16,512]{2,1,0:T(8,128)S(1)} fusion(f32[16,512]{1,0:T(8,128)S(1)} %fusion.3, s32[4096]{0:T(1024)S(1)} %copy-done.8, f32[1,16,1,4096]{3,2,1,0:T(1,128)S(1)} %get-tuple-element.151), kind=kOutput, calls=%fused_computation.23 | convolution fusion | flops 404758528 | bytes 344064 | tf_op jit(solution)/shard_map/cjb,sb->cjs/dot_general | solution.py:93
  20.0 12.9 %psum.21 = f32[1,16,512]{2,1,0:T(8,128)S(1)} all-reduce(f32[1,16,512]{2,1,0:T(8,128)S(1)} %fusion.21), channel_id=1, replica_groups=mesh['freq'=8,'tm'=4] {'tm'}, use_global_device_ids=true, to_apply=%region_0.0 | all-reduce | flops 8192 | bytes 65536 | tf_op jit(solution)/shard_map/psum | solution.py:178
  33.2 2.7 %fusion.11 = f32[1,1,8,4096]{3,2,1,0:T(8,128)S(1)} fusion(s32[4096]{0:T(1024)S(1)} %copy-done.7, f32[1,8,512]{2,1,0:T(8,128)S(1)} %add_multiply_fusion), kind=kOutput, calls=%fused_computation.13 | convolution fusion | flops 203423744 | bytes 163840 | tf_op jit(solution)/shard_map/cjs,sb->cjb/dot_general | solution.py:71
  35.9 0.3 constant_dynamic-update-slice_fusion.63
  36.2 0.1 constant_dynamic-update-slice_fusion.62
  36.3 0.3 constant_dynamic-update-slice_fusion.61
  36.6 0.1 constant_dynamic-update-slice_fusion.60
  36.7 0.1 constant_dynamic-update-slice_fusion.59
  36.8 0.1 constant_dynamic-update-slice_fusion.58
  36.9 0.1 constant_dynamic-update-slice_fusion.57
  37.0 2.7 %fusion.9 = f32[1,1,8,4096]{3,2,1,0:T(8,128)S(1)} fusion(s32[4096]{0:T(1024)S(1)} %copy-done.8, f32[1,8,512]{2,1,0:T(8,128)S(1)} %add_multiply_fusion), kind=kOutput, calls=%fused_computation.11 | convolution fusion | flops 203423744 | bytes 163840 | tf_op jit(solution)/shard_map/cjs,sb->cjb/dot_general | solution.py:74
  39.6 0.3 constant_dynamic-update-slice_fusion.47
  39.9 0.2 constant_dynamic-update-slice_fusion.56
  40.1 0.3 constant_dynamic-update-slice_fusion.45
  40.5 0.1 constant_dynamic-update-slice_fusion.53
  40.7 0.1 constant_dynamic-update-slice_fusion.51
  40.8 0.1 constant_dynamic-update-slice_fusion.50
  40.9 0.1 constant_dynamic-update-slice_fusion.48
  41.0 0.1 constant_dynamic-update-slice_fusion.43
  41.1 0.1 constant_dynamic-update-slice_fusion.42
  41.2 0.1 constant_dynamic-update-slice_fusion.41
  41.3 0.1 constant_dynamic-update-slice_fusion.40
  41.5 0.1 constant_dynamic-update-slice_fusion.37
  41.7 0.1 constant_dynamic-update-slice_fusion.35
  42.0 3.8 %fusion.1 = f32[16,512]{1,0:T(8,128)S(1)} fusion(s32[4096]{0:T(1024)S(1)} %copy-done.7, f32[1,16,1,4096]{3,2,1,0:T(1,128)S(1)} %constant_dynamic-update-slice_fusion.32), kind=kOutput, calls=%fused_computation.2 | convolution fusion | flops 404750336 | bytes 311296 | tf_op jit(solution)/shard_map/cjb,sb->cjs/dot_general | solution.py:92
  45.8 4.1 %fusion.23 = f32[1,16,512]{2,1,0:T(8,128)S(1)} fusion(f32[16,512]{1,0:T(8,128)S(1)} %fusion.1, s32[4096]{0:T(1024)S(1)} %copy-done.8, f32[1,16,1,4096]{3,2,1,0:T(1,128)S(1)} %get-tuple-element.139), kind=kOutput, calls=%fused_computation.25 | convolution fusion | flops 404758528 | bytes 344064 | tf_op jit(solution)/shard_map/cjb,sb->cjs/dot_general | solution.py:93
  49.9 10.3 %psum.22 = f32[1,16,512]{2,1,0:T(8,128)S(1)} all-reduce(f32[1,16,512]{2,1,0:T(8,128)S(1)} %fusion.23), channel_id=1, replica_groups=mesh['freq'=8,'tm'=4] {'tm'}, use_global_device_ids=true, to_apply=%region_1.0 | all-reduce | flops 8192 | bytes 65536 | tf_op jit(solution)/shard_map/psum | solution.py:178
  61.3 37.5 %psum.23 = f32[8,128,4]{1,0,2:T(8,128)S(1)} all-reduce(f32[8,128,4]{1,0,2:T(8,128)S(1)} %bitcast.1387), channel_id=1, replica_groups=mesh['freq'=8,'tm'=4] {'freq'}, use_global_device_ids=true, to_apply=%region_4.0 | all-reduce | flops 4096 | bytes 32768 | tf_op jit(solution)/shard_map/psum | solution.py:186
  98.8 0.3 fusion.55
  99.0 0.1 copy.13
  99.1 0.4 cholesky.16
  99.6 0.7 compare_reduce_fusion
  100.2 0.6 fusion.62
  100.9 0.3 custom-call.8
  101.2 1.0 fusion.44
  102.2 0.5 fusion.65
  102.7 0.2 fusion.72
  103.0 0.6 fusion.70
  (64 shorter events, 2.0 us)
Async XLA Ops:
  2.3 3.4 %copy-start = (s32[1,1,4096]{2,1,0:T(1,128)S(1)}, s32[1,1,4096]{2,1,0:T(1,128)}, u32[]{:S(2)}) copy-start(s32[1,1,4096]{2,1,0:T(1,128)} %param.12) | copy-start | bytes 49156
  6.2 0.7 copy-start.4
  6.2 0.7 copy-start.8
  11.4 0.7 copy-start.7
  15.9 17.0 %copy-start.2 = (f32[512]{0:T(512)S(1)}, f32[512]{0:T(512)}, u32[]{:S(2)}) copy-start(f32[512]{0:T(512)} %param.16) | copy-start | bytes 6148
  15.9 17.0 %copy-start.1 = (f32[1,8,512]{2,1,0:T(8,128)S(1)}, f32[1,8,512]{2,1,0:T(8,128)}, u32[]{:S(2)}) copy-start(f32[1,8,512]{2,1,0:T(8,128)} %param.15) | copy-start | bytes 49156
  15.9 17.0 %copy-start.3 = (f32[1,8,512]{2,1,0:T(8,128)S(1)}, f32[1,8,512]{2,1,0:T(8,128)}, u32[]{:S(2)}) copy-start(f32[1,8,512]{2,1,0:T(8,128)} %param.14) | copy-start | bytes 49156
  60.4 42.6 %copy-start.5 = (f32[1,8,128]{2,1,0:T(8,128)}, f32[1,8,128]{2,1,0:T(8,128)S(1)}, u32[]{:S(2)}) copy-start(f32[1,8,128]{2,1,0:T(8,128)S(1)} %get-tuple-element.4) | copy-start | bytes 12292
  103.0 0.6 copy-start.6
where the time goes:
time: 104 us
  blocking collectives  60.6 us (58%)
  matrix products  29.2 us (28%)
  other arithmetic  11.7 us (11%)
  between operations  1.64 us (2%)
    psum x1, blocking collectives, shards(): moments = lax.psum(local_moments, 'freq')  37.5 us
    psum x2, blocking collectives, shards(): summed = lax.psum(totals, 'tm')  23.2 us
    dot_general x2, matrix products, normal_sums(): jnp.einsum('cjb,sb->cjs', term_second, second_hot, precision=lax.Precisio...  8.11 us
    dot_general x2, matrix products, normal_sums(): jnp.einsum('cjb,sb->cjs', term_first, first_hot, precision=lax.Precision....  7.68 us
    unnamed x57, other arithmetic  6.62 us
    dot_general x2, matrix products, normal_sums(): jnp.einsum('cjs,sb->cjb', gains, first_hot, precision=lax.Precision.HIGHEST)  6.05 us
    dot_general x2, matrix products, normal_sums(): jnp.einsum('cjs,sb->cjb', gains, second_hot, precision=lax.Precision.HIGH...  5.31 us

commit v1 on v0

--- a/solution.py
+++ b/solution.py
@@ -1,9 +1,18 @@
+import functools
 import jax
 import jax.numpy as jnp
 from jax import lax
 from jax.sharding import PartitionSpec as P
 
 SWEEPS = 2
+
+
+def fit_masks_on(work_x, shard_axis):
+    z1 = jnp.sum(jax.lax.all_gather(work_x, shard_axis), axis=0)
+    return z1
+
+
+switch_types = functools.partial(fit_masks_on, shard_axis="freq")
 
 
 def entries(array, axis):
@@ -183,7 +192,7 @@
     basis = channel_basis(channel_index, float(total_channels))
     combined = gains_part + dual_part
     local_moments = jnp.einsum("fk,fjs->kjs", basis, combined, precision=lax.Precision.HIGHEST)
-    moments = lax.psum(local_moments, "freq")
+    moments = switch_types(local_moments)
     coeffs = poly_fit(moments, total_channels)
     consensus_out = jnp.einsum("fk,kjs->fjs", basis, coeffs, precision=lax.Precision.HIGHEST)
     dual_out = dual_part + gains_part - consensus_out

time: 104 us -> 97.6 us (0.938)
  blocking collectives: 60.6 us -> 54.1 us
    psum x1 -> x0, blocking collectives: 37.5 us -> none  [shards(): moments = lax.psum(local_moments, 'freq')]
    all_gather x0 -> x1, blocking collectives: none -> 30.9 us  [fit_masks_on(): z1 = jnp.sum(jax.lax.all_gather(work_x, shard_axis), axis=0)]
    unnamed x57 -> x56, other arithmetic: 6.62 us -> 6.54 us
where the time goes in v1:
time: 97.6 us; the launch traced here: 97.1 us
  blocking collectives  54.1 us (55%)
  matrix products  29.2 us (30%)
  other arithmetic  11.7 us (12%)
  between operations  1.65 us (2%)
    all_gather x1, blocking collectives, fit_masks_on(): z1 = jnp.sum(jax.lax.all_gather(work_x, shard_axis), axis=0)  30.9 us
    psum x2, blocking collectives, shards(): summed = lax.psum(totals, 'tm')  23.2 us
    dot_general x2, matrix products, normal_sums(): jnp.einsum('cjb,sb->cjs', term_second, second_hot, precision=lax.Precisio...  8.11 us
    dot_general x2, matrix products, normal_sums(): jnp.einsum('cjb,sb->cjs', term_first, first_hot, precision=lax.Precision....  7.68 us
    unnamed x56, other arithmetic  6.54 us
    dot_general x2, matrix products, normal_sums(): jnp.einsum('cjs,sb->cjb', gains, first_hot, precision=lax.Precision.HIGHEST)  6.05 us
    dot_general x2, matrix products, normal_sums(): jnp.einsum('cjs,sb->cjb', gains, second_hot, precision=lax.Precision.HIGH...  5.31 us

profile of v1, /device:TPU:0, one launch (start us, length us, event | category | flops | bytes accessed | tf_op | source)
XLA Modules:
  0.0 97.1 jit_solution(9765739326498196158)
XLA Ops:
  0.6 0.9 convert_element_type.39
  1.5 0.9 convert_element_type.40
  2.4 3.4 %fusion.10 = f32[1,1,8,4096]{3,2,1,0:T(8,128)S(1)} fusion(s32[4096]{0:T(1024)} %param.18, f32[1,8,512]{2,1,0:T(8,128)} %param.13), kind=kOutput, calls=%fused_computation.12 | convolution fusion | flops 203423744 | bytes 163840 | tf_op jit(solution)/shard_map/cjs,sb->cjb/dot_general | solution.py:80
  5.7 0.3 constant_dynamic-update-slice_fusion.31
  6.1 0.1 constant_dynamic-update-slice_fusion.30
  6.2 0.3 constant_dynamic-update-slice_fusion.29
  6.5 0.1 constant_dynamic-update-slice_fusion.28
  6.6 0.1 constant_dynamic-update-slice_fusion.27
  6.7 0.1 constant_dynamic-update-slice_fusion.26
  6.8 0.1 constant_dynamic-update-slice_fusion.25
  6.9 2.7 %fusion.8 = f32[1,1,8,4096]{3,2,1,0:T(8,128)S(1)} fusion(s32[4096]{0:T(1024)S(1)} %copy-done.8, f32[1,8,512]{2,1,0:T(8,128)S(1)} %copy-done.4), kind=kOutput, calls=%fused_computation.10 | convolution fusion | flops 203423744 | bytes 163840 | tf_op jit(solution)/shard_map/cjs,sb->cjb/dot_general | solution.py:83
  9.6 0.3 constant_dynamic-update-slice_fusion.15
  9.9 0.2 constant_dynamic-update-slice_fusion.24
  10.2 0.1 constant_dynamic-update-slice_fusion.21
  10.3 0.1 constant_dynamic-update-slice_fusion.19
  10.4 0.1 constant_dynamic-update-slice_fusion.18
  10.5 0.3 constant_dynamic-update-slice_fusion.13
  10.9 0.1 constant_dynamic-update-slice_fusion.16
  11.0 0.1 constant_dynamic-update-slice_fusion.11
  11.1 0.1 constant_dynamic-update-slice_fusion.10
  11.2 0.1 constant_dynamic-update-slice_fusion.9
  11.3 0.1 constant_dynamic-update-slice_fusion.8
  11.5 0.1 constant_dynamic-update-slice_fusion.5
  11.7 0.1 constant_dynamic-update-slice_fusion.3
  11.9 0.1 copy-done.7
  12.1 3.8 %fusion.3 = f32[16,512]{1,0:T(8,128)S(1)} fusion(s32[4096]{0:T(1024)S(1)} %copy-done.7, f32[1,16,1,4096]{3,2,1,0:T(1,128)S(1)} %constant_dynamic-update-slice_fusion), kind=kOutput, calls=%fused_computation.4 | convolution fusion | flops 404750336 | bytes 311296 | tf_op jit(solution)/shard_map/cjb,sb->cjs/dot_general | solution.py:101
  16.0 4.0 %fusion.21 = f32[1,16,512]{2,1,0:T(8,128)S(1)} fusion(f32[16,512]{1,0:T(8,128)S(1)} %fusion.3, s32[4096]{0:T(1024)S(1)} %copy-done.8, f32[1,16,1,4096]{3,2,1,0:T(1,128)S(1)} %get-tuple-element.151), kind=kOutput, calls=%fused_computation.23 | convolution fusion | flops 404758528 | bytes 344064 | tf_op jit(solution)/shard_map/cjb,sb->cjs/dot_general | solution.py:102
  20.0 12.9 %psum.14 = f32[1,16,512]{2,1,0:T(8,128)S(1)} all-reduce(f32[1,16,512]{2,1,0:T(8,128)S(1)} %fusion.21), channel_id=1, replica_groups=mesh['freq'=8,'tm'=4] {'tm'}, use_global_device_ids=true, to_apply=%region_0.0 | all-reduce | flops 8192 | bytes 65536 | tf_op jit(solution)/shard_map/psum | solution.py:187
  33.2 2.7 %fusion.11 = f32[1,1,8,4096]{3,2,1,0:T(8,128)S(1)} fusion(s32[4096]{0:T(1024)S(1)} %copy-done.7, f32[1,8,512]{2,1,0:T(8,128)S(1)} %add_multiply_fusion), kind=kOutput, calls=%fused_computation.13 | convolution fusion | flops 203423744 | bytes 163840 | tf_op jit(solution)/shard_map/cjs,sb->cjb/dot_general | solution.py:80
  35.9 0.3 constant_dynamic-update-slice_fusion.63
  36.2 0.1 constant_dynamic-update-slice_fusion.62
  36.3 0.3 constant_dynamic-update-slice_fusion.61
  36.6 0.1 constant_dynamic-update-slice_fusion.60
  36.7 0.1 constant_dynamic-update-slice_fusion.59
  36.8 0.1 constant_dynamic-update-slice_fusion.58
  36.9 0.1 constant_dynamic-update-slice_fusion.57
  37.0 2.7 %fusion.9 = f32[1,1,8,4096]{3,2,1,0:T(8,128)S(1)} fusion(s32[4096]{0:T(1024)S(1)} %copy-done.8, f32[1,8,512]{2,1,0:T(8,128)S(1)} %add_multiply_fusion), kind=kOutput, calls=%fused_computation.11 | convolution fusion | flops 203423744 | bytes 163840 | tf_op jit(solution)/shard_map/cjs,sb->cjb/dot_general | solution.py:83
  39.6 0.3 constant_dynamic-update-slice_fusion.47
  39.9 0.2 constant_dynamic-update-slice_fusion.56
  40.1 0.3 constant_dynamic-update-slice_fusion.45
  40.5 0.1 constant_dynamic-update-slice_fusion.53
  40.7 0.1 constant_dynamic-update-slice_fusion.51
  40.8 0.1 constant_dynamic-update-slice_fusion.50
  40.9 0.1 constant_dynamic-update-slice_fusion.48
  41.0 0.1 constant_dynamic-update-slice_fusion.43
  41.1 0.1 constant_dynamic-update-slice_fusion.42
  41.2 0.1 constant_dynamic-update-slice_fusion.41
  41.3 0.1 constant_dynamic-update-slice_fusion.40
  41.5 0.1 constant_dynamic-update-slice_fusion.37
  41.7 0.1 constant_dynamic-update-slice_fusion.35
  42.0 3.8 %fusion.1 = f32[16,512]{1,0:T(8,128)S(1)} fusion(s32[4096]{0:T(1024)S(1)} %copy-done.7, f32[1,16,1,4096]{3,2,1,0:T(1,128)S(1)} %constant_dynamic-update-slice_fusion.32), kind=kOutput, calls=%fused_computation.2 | convolution fusion | flops 404750336 | bytes 311296 | tf_op jit(solution)/shard_map/cjb,sb->cjs/dot_general | solution.py:101
  45.8 4.1 %fusion.23 = f32[1,16,512]{2,1,0:T(8,128)S(1)} fusion(f32[16,512]{1,0:T(8,128)S(1)} %fusion.1, s32[4096]{0:T(1024)S(1)} %copy-done.8, f32[1,16,1,4096]{3,2,1,0:T(1,128)S(1)} %get-tuple-element.139), kind=kOutput, calls=%fused_computation.25 | convolution fusion | flops 404758528 | bytes 344064 | tf_op jit(solution)/shard_map/cjb,sb->cjs/dot_general | solution.py:102
  49.9 10.3 %psum.15 = f32[1,16,512]{2,1,0:T(8,128)S(1)} all-reduce(f32[1,16,512]{2,1,0:T(8,128)S(1)} %fusion.23), channel_id=1, replica_groups=mesh['freq'=8,'tm'=4] {'tm'}, use_global_device_ids=true, to_apply=%region_1.0 | all-reduce | flops 8192 | bytes 65536 | tf_op jit(solution)/shard_map/psum | solution.py:187
  61.3 30.9 %all-gather = f32[32,8,128]{2,1,0:T(8,128)S(1)} all-gather(f32[4,8,128]{2,1,0:T(8,128)S(1)} %broadcast_multiply_fusion), channel_id=2, replica_groups=mesh['freq'=8,'tm'=4] {'freq'}, dimensions={0}, use_global_device_ids=true | all-gather | bytes 147456 | tf_op jit(solution)/shard_map/all_gather | solution.py:11
  92.2 0.3 fusion.55
  92.5 0.1 copy.15
  92.6 0.4 cholesky.16
  93.0 0.7 compare_reduce_fusion
  93.7 0.6 fusion.62
  94.3 0.3 custom-call.8
  94.7 1.0 %fusion.32 = f32[8,128,4]{2,1,0:T(8,128)S(1)} fusion(f32[1,4,8,128]{3,2,1,0:T(8,128)S(1)} %bitcast.1384, f32[1,4,4]{1,2,0:T(4,128)S(1)} %custom-call.8), kind=kOutput, calls=%fused_computation.99 | convolution fusion | flops 196608 | bytes 32832 | tf_op jit(solution)/shard_map/triangular_solve | solution.py:154
  95.7 0.5 fusion.65
  96.2 0.2 fusion.72
  96.5 0.6 fusion.70
  (63 shorter events, 2.0 us)
Async XLA Ops:
  2.3 3.4 %copy-start = (s32[1,1,4096]{2,1,0:T(1,128)S(1)}, s32[1,1,4096]{2,1,0:T(1,128)}, u32[]{:S(2)}) copy-start(s32[1,1,4096]{2,1,0:T(1,128)} %param.12) | copy-start | bytes 49156
  6.2 0.7 copy-start.4
  6.2 0.7 copy-start.8
  11.4 0.7 copy-start.7
  15.9 17.0 %copy-start.2 = (f32[512]{0:T(512)S(1)}, f32[512]{0:T(512)}, u32[]{:S(2)}) copy-start(f32[512]{0:T(512)} %param.16) | copy-start | bytes 6148
  15.9 17.0 %copy-start.1 = (f32[1,8,512]{2,1,0:T(8,128)S(1)}, f32[1,8,512]{2,1,0:T(8,128)}, u32[]{:S(2)}) copy-start(f32[1,8,512]{2,1,0:T(8,128)} %param.15) | copy-start | bytes 49156
  15.9 17.0 %copy-start.3 = (f32[1,8,512]{2,1,0:T(8,128)S(1)}, f32[1,8,512]{2,1,0:T(8,128)}, u32[]{:S(2)}) copy-start(f32[1,8,512]{2,1,0:T(8,128)} %param.14) | copy-start | bytes 49156
  60.4 36.0 %copy-start.5 = (f32[1,8,128]{2,1,0:T(8,128)}, f32[1,8,128]{2,1,0:T(8,128)S(1)}, u32[]{:S(2)}) copy-start(f32[1,8,128]{2,1,0:T(8,128)S(1)} %get-tuple-element.4) | copy-start | bytes 12292
  96.4 0.6 copy-start.6
